TPU v7x, 32 devices: a whole 2x2x4 slice. The times are simulated.
32 devices in a mesh: dp: 8 (over z, core), mp: 4 (over y, x).
Axes of the slice: x: 2, y: 2, z: 4, core: 2. Of those that a mesh axis runs over, the one named last changes fastest.
Arguments:
- momentum: float32 [8, 256, 5120], P('dp', 'mp'), may hold values from -60 to 60
- gradient: bfloat16 [8, 256, 5120], P('dp', 'mp'), may hold values from -60 to 60
- columns: int32 [256], replicated, may hold values from 0 to 5119, as said below
Outputs:
- update: bfloat16 [256, 5120], P('mp', 'dp')
- new_momentum: float32 [8, 256, 5120], P('dp', 'mp')
Inputs may be any that keep to these rules, and one draw needn't show every extreme that they name: `columns`: 256 distinct frequencies, 0 and 5119 always among them, in no particular order.
All inputs are finite; a program needn't handle non-finite values.
Results may differ from a plain program's by a relative error of at most 0.007.
Values may be sent and summed in bfloat16 or wider, within the bound.
A program may use at most 64 MiB of HBM per device.

v0:
```python
import math
import jax
import jax.numpy as jnp
from jax import lax
from jax.sharding import PartitionSpec as P

COLS = 5120
RANK = 256
ITERS = 5
inertia = 0.9
linear_term = 3.4445
cubic_term = -4.775
quintic_term = 2.0315


def dct_table(columns):
    positions = jnp.arange(COLS, dtype=jnp.int32)
    phase_index = (2 * positions[:, None] + 1) * columns[None, :] % (4 * COLS)
    angles = phase_index.astype(jnp.float32) * (math.pi / (2 * COLS))
    column_scale = jnp.where(columns == 0, math.sqrt(1.0 / COLS), math.sqrt(2.0 / COLS))
    return (jnp.cos(angles) * column_scale[None, :]).astype(jnp.bfloat16)


def orthogonalize(gram_matrix):
    squared_norm = jnp.trace(gram_matrix) + 1e-06
    inverse_norm = 1.0 / jnp.sqrt(squared_norm)
    identity = jnp.eye(gram_matrix.shape[0], dtype=jnp.float32)
    gram_now = gram_matrix * (inverse_norm * inverse_norm)
    mixing = identity * inverse_norm
    highest = lax.Precision.HIGHEST
    for _ in range(ITERS):
        polynomial = (
            linear_term * identity
            + cubic_term * gram_now
            + quintic_term * jnp.dot(gram_now, gram_now, precision=highest)
        )
        mixing = jnp.dot(mixing, polynomial, precision=highest)
        gram_now = jnp.dot(
            jnp.dot(polynomial, gram_now, precision=highest), polynomial, precision=highest
        )
    return mixing


def body(momentum, gradient, columns):
    highest = lax.Precision.HIGHEST
    cosines = dct_table(columns)
    current = inertia * momentum[0] + gradient[0].astype(jnp.float32)
    partial_value = jnp.dot(
        current.astype(jnp.bfloat16), cosines, preferred_element_type=jnp.float32
    )
    replica_count = lax.axis_size("dp")
    summed = lax.psum(partial_value, "dp") / replica_count
    coded_rows = summed.astype(jnp.bfloat16)
    block_rows = lax.all_gather(summed, "mp", axis=0, tiled=True)
    gram_matrix = jnp.dot(block_rows.T, block_rows, precision=highest)
    mixing = orthogonalize(gram_matrix)
    orthogonal = jnp.dot(summed, mixing, precision=highest).astype(jnp.bfloat16)
    decoded = jnp.dot(coded_rows, cosines.T, preferred_element_type=jnp.float32)
    band_width = COLS // replica_count
    band_start = lax.axis_index("dp") * band_width
    band_cosines = lax.dynamic_slice_in_dim(cosines, band_start, band_width, 0)
    direction = jnp.dot(orthogonal, band_cosines.T, preferred_element_type=jnp.float32)
    row_count = momentum.shape[1] * lax.axis_size("mp")
    update = (direction * math.sqrt(row_count * COLS / RANK)).astype(jnp.bfloat16)
    new_momentum = (current - decoded)[None]
    return (update, new_momentum)


def solution(mesh):
    return jax.shard_map(
        body,
        mesh=mesh,
        in_specs=(P("dp", "mp", None), P("dp", "mp", None), P()),
        out_specs=(P("mp", "dp"), P("dp", "mp", None)),
        check_vma=False,
    )
```

profile of v0, /device:TPU:0, one launch (start us, length us, event | category | flops | bytes accessed | tf_op | source)
XLA Modules:
  0.0 141.9 jit_solution(5607261184913191640)
XLA Ops:
  7.2 0.7 compare_select_fusion
  7.9 25.8 %fusion.15 = f32[64,256]{1,0:T(8,128)} fusion(bf16[1,64,5120]{2,1,0:T(8,128)(2,1)} %param.4, f32[1,64,5120]{2,1,0:T(8,128)} %param.3, f32[256]{0:T(256)S(1)} %compare_select_fusion, s32[256]{0:T(256)} %param.5, s32[5120]{0:T(1024)S(1)} %multiply_add_fusion), kind=kOutput, calls=%fused_computation.27 | convolution fusion | flops 183500800 | bytes 2054144 | tf_op jit(solution)/shard_map/dot_general | solution.py:48
  33.7 22.0 %fusion.5 = bf16[5120,256]{1,0:T(8,128)(2,1)S(1)} fusion(f32[256]{0:T(256)S(1)} %compare_select_fusion, s32[256]{0:T(256)S(1)} %copy-done.1, s32[5120]{0:T(1024)S(1)} %multiply_add_fusion), kind=kLoop, calls=%fused_computation.7 | loop fusion | flops 14417920 | bytes 2643968 | tf_op jit(solution)/shard_map/convert_element_type | solution.py:21
  55.8 35.5 %all-reduce.2.cloned.1.call-done = f32[64,256]{1,0:T(8,128)} async-done(((f32[64,256]{1,0:T(8,128)}), f32[64,256]{1,0:T(8,128)}) %all-reduce.2.cloned.1.call-update) | async-done | bytes 65552 | tf_op jit(solution)/shard_map/psum | solution.py:52
  91.3 0.8 broadcast_multiply_fusion
  92.1 9.5 %all_gather.3 = f32[256,256]{1,0:T(8,128)S(1)} all-gather(f32[64,256]{1,0:T(8,128)S(1)} %broadcast_multiply_fusion), channel_id=1, replica_groups=mesh['dp'=8,'mp'=4] {'mp'}, dimensions={0}, use_global_device_ids=true | all-gather | bytes 327680 | tf_op jit(solution)/shard_map/all_gather | solution.py:54
  101.6 1.2 select_reduce_fusion
  103.5 0.4 fusion.13
  103.9 0.4 fusion.21
  104.7 0.4 fusion.39
  105.1 0.4 fusion.12
  105.8 0.4 fusion.42
  106.2 0.4 fusion.11
  106.6 0.4 fusion.44
  107.0 0.4 fusion.45
  107.4 0.4 fusion.10
  107.8 0.4 fusion.47
  108.2 0.4 fusion.48
  108.6 0.4 fusion.9
  109.0 0.4 fusion.40
  109.4 0.4 fusion.43
  110.1 0.4 fusion.49
  110.8 0.9 fusion.14
  111.7 23.3 %fusion = f32[1,64,5120]{2,1,0:T(8,128)} fusion(bf16[1,64,5120]{2,1,0:T(8,128)(2,1)S(1)} %copy-done.3, f32[1,64,5120]{2,1,0:T(8,128)S(1)} %copy-done.2, f32[256]{0:T(256)S(1)} %compare_select_fusion, s32[256]{0:T(256)S(1)} %copy-done.1, s32[5120]{0:T(1024)S(1)} %multiply_add_fusion, f32[64,256]{1,0:T(8,128)S(1)} %copy-done), kind=kOutput, calls=%fused_computation.2 | convolution fusion | flops 183533568 | bytes 3364864 | tf_op jit(solution)/shard_map/dot_general | solution.py:58
  (15 shorter events, 1.5 us)
Async XLA Ops:
  7.2 84.1 %all-reduce.2.cloned.1.call-start = ((), (), s32[]{:S(2)}) async-start(), calls=%async_computation | async-start | bytes 131072 | tf_op jit(solution)/shard_map/psum | solution.py:52
  7.9 25.8 %copy-start.1 = (s32[256]{0:T(256)S(1)}, s32[256]{0:T(256)}, u32[]{:S(2)}) copy-start(s32[256]{0:T(256)} %param.5) | copy-start | bytes 3076
  107.8 2.7 %copy-start = (f32[64,256]{1,0:T(8,128)S(1)}, f32[64,256]{1,0:T(8,128)}, u32[]{:S(2)}) copy-start(f32[64,256]{1,0:T(8,128)} %all-reduce.2.cloned.1.call-done) | copy-start | bytes 196612
  108.2 3.5 %copy-start.2 = (f32[1,64,5120]{2,1,0:T(8,128)S(1)}, f32[1,64,5120]{2,1,0:T(8,128)}, u32[]{:S(2)}) copy-start(f32[1,64,5120]{2,1,0:T(8,128)} %param.3) | copy-start | bytes 3932164
  108.2 3.5 %copy-start.3 = (bf16[1,64,5120]{2,1,0:T(8,128)(2,1)S(1)}, bf16[1,64,5120]{2,1,0:T(8,128)(2,1)}, u32[]{:S(2)}) copy-start(bf16[1,64,5120]{2,1,0:T(8,128)(2,1)} %param.4) | copy-start | bytes 1966084
Sparse Core Ops, SparseCore 0:
  33.8 57.4 all-reduce.1
where the time goes:
time: 142 us
  matrix products  58.3 us (41%)
  waiting for transfers between devices  35.5 us (25%)
  other arithmetic  23.6 us (17%)
  between operations  14.9 us (10%)
  blocking collectives  9.46 us (7%)
    psum x1, waiting for transfers between devices, body(): summed = lax.psum(partial_value, 'dp') / replica_count  35.5 us
    dot_general x1, matrix products, body(): jnp.dot(current.astype(jnp.bfloat16), cosines, preferred_element_type=jnp...  25.8 us
    dot_general x1, matrix products, body(): decoded = jnp.dot(coded_rows, cosines.T, preferred_element_type=jnp.float32)  23.3 us
    convert_element_type x1, other arithmetic, dct_table(): return (jnp.cos(angles) * column_scale[None, :]).astype(jnp.bfloat16)  22 us
    all_gather x1, blocking collectives, body(): block_rows = lax.all_gather(summed, 'mp', axis=0, tiled=True)  9.46 us
  transfers between devices with their start and end apart: 1, of which 1 were waited for; matrix products, arithmetic and copies ran while one was open for 16% of the time, Pallas kernels for 0%

commit v1 on v0

--- a/solution.py
+++ b/solution.py
@@ -51,7 +51,12 @@
     replica_count = lax.axis_size("dp")
     summed = lax.psum(partial_value, "dp") / replica_count
     coded_rows = summed.astype(jnp.bfloat16)
-    block_rows = lax.all_gather(summed, "mp", axis=0, tiled=True)
+    ring = [summed]
+    for hop in range(3):
+        ring.append(lax.ppermute(ring[-1], "mp", [(dev, (dev + 1) % 4) for dev in range(4)]))
+    block_rows = jnp.roll(
+        jnp.concatenate(ring[::-1], axis=0), (lax.axis_index("mp") + 1) * ring[0].shape[0], axis=0
+    )
     gram_matrix = jnp.dot(block_rows.T, block_rows, precision=highest)
     mixing = orthogonalize(gram_matrix)
     orthogonal = jnp.dot(summed, mixing, precision=highest).astype(jnp.bfloat16)

time: 142 us -> 164 us (1.15)
  waiting for transfers between devices: 35.5 us -> 61.3 us
  blocking collectives: 9.46 us -> 0 us
  starting transfers between devices: 0.04 us -> 4.68 us
    psum x1, waiting for transfers between devices: 35.5 us -> 57.6 us  [body(): summed = lax.psum(partial_value, 'dp') / replica_count]
    all_gather x1 -> x0, blocking collectives: 9.46 us -> none  [body(): block_rows = lax.all_gather(summed, 'mp', axis=0, tiled=True)]
    ppermute x0 -> x3, starting transfers between devices: none -> 4.64 us  [body(): lax.ppermute(ring[-1], 'mp', [(dev, (dev + 1) % 4) for dev in range(4)])]
    ppermute x0 -> x3, waiting for transfers between devices: none -> 3.7 us  [body(): lax.ppermute(ring[-1], 'mp', [(dev, (dev + 1) % 4) for dev in range(4)])]
  transfers between devices with their start and end apart: 1 -> 4, of which waited for: 1 -> 2; matrix products, arithmetic and copies ran while one was open for 16% -> 28% of each run, Pallas kernels for 0% -> 0%
where the time goes in v1:
time: 164 us
  waiting for transfers between devices  61.3 us (37%)
  matrix products  59.2 us (36%)
  other arithmetic  23.6 us (14%)
  between operations  15 us (9%)
  starting transfers between devices  4.68 us (3%)
    psum x1, waiting for transfers between devices, body(): summed = lax.psum(partial_value, 'dp') / replica_count  57.6 us
    dot_general x1, matrix products, body(): jnp.dot(current.astype(jnp.bfloat16), cosines, preferred_element_type=jnp...  25.8 us
    dot_general x1, matrix products, body(): decoded = jnp.dot(coded_rows, cosines.T, preferred_element_type=jnp.float32)  24.3 us
    convert_element_type x1, other arithmetic, dct_table(): return (jnp.cos(angles) * column_scale[None, :]).astype(jnp.bfloat16)  22 us
    ppermute x3, starting transfers between devices, body(): lax.ppermute(ring[-1], 'mp', [(dev, (dev + 1) % 4) for dev in range(4)])  4.64 us
    ppermute x3, waiting for transfers between devices, body(): lax.ppermute(ring[-1], 'mp', [(dev, (dev + 1) % 4) for dev in range(4)])  3.7 us
  transfers between devices with their start and end apart: 4, of which 2 were waited for; matrix products, arithmetic and copies ran while one was open for 28% of the time, Pallas kernels for 0%

profile of v1, /device:TPU:0, one launch (start us, length us, event | category | flops | bytes accessed | tf_op | source)
XLA Modules:
  0.0 163.9 jit_solution(4000104963032374002)
XLA Ops:
  7.2 0.7 compare_select_fusion
  7.9 25.8 %fusion.15 = f32[64,256]{1,0:T(8,128)} fusion(bf16[1,64,5120]{2,1,0:T(8,128)(2,1)} %param.4, f32[1,64,5120]{2,1,0:T(8,128)} %param.3, f32[256]{0:T(256)S(1)} %compare_select_fusion, s32[256]{0:T(256)} %param.5, s32[5120]{0:T(1024)S(1)} %multiply_add_fusion), kind=kOutput, calls=%fused_computation.27 | convolution fusion | flops 183500800 | bytes 2054144 | tf_op jit(solution)/shard_map/dot_general | solution.py:48
  33.7 57.6 %all-reduce.2.cloned.1.call-done = f32[64,256]{1,0:T(8,128)} async-done(((f32[64,256]{1,0:T(8,128)}), f32[64,256]{1,0:T(8,128)}) %all-reduce.2.cloned.1.call-update) | async-done | bytes 65552 | tf_op jit(solution)/shard_map/psum | solution.py:52
  91.3 0.9 broadcast_multiply_fusion
  92.2 1.5 collective-permute-start
  93.7 3.7 %collective-permute-done = f32[64,256]{1,0:T(8,128)S(1)} collective-permute-done((f32[64,256]{1,0:T(8,128)S(1)}, f32[64,256]{1,0:T(8,128)S(1)}, u32[]{:S(2)}, u32[]{:S(2)}) %collective-permute-start) | collective-permute-done | bytes 65568 | tf_op jit(solution)/shard_map/ppermute | solution.py:56
  97.4 1.0 collective-permute-start.1
  98.4 22.0 %fusion.5 = bf16[5120,256]{1,0:T(8,128)(2,1)S(1)} fusion(f32[256]{0:T(256)S(1)} %compare_select_fusion, s32[256]{0:T(256)S(1)} %copy-done.1, s32[5120]{0:T(1024)S(1)} %multiply_add_fusion), kind=kLoop, calls=%fused_computation.7 | loop fusion | flops 14417920 | bytes 2643968 | tf_op jit(solution)/shard_map/convert_element_type | solution.py:21
  120.5 2.2 %collective-permute-start.2 = (f32[64,256]{1,0:T(8,128)S(1)}, f32[64,256]{1,0:T(8,128)S(1)}, u32[]{:S(2)}, u32[]{:S(2)}) collective-permute-start(f32[64,256]{1,0:T(8,128)S(1)} %collective-permute-done.1), channel_id=1, source_target_pairs={{0,1},{1,2},{2,3},{3,0},{4,5},{5,6},{6,7},{7,4},{8,9},{9,10},{10,1... | collective-permute-start | bytes 196616 | tf_op jit(solution)/shard_map/ppermute | solution.py:56
  122.6 24.3 %fusion = f32[1,64,5120]{2,1,0:T(8,128)} fusion(bf16[1,64,5120]{2,1,0:T(8,128)(2,1)S(1)} %copy-done.2, f32[1,64,5120]{2,1,0:T(8,128)} %param.3, f32[256]{0:T(256)S(1)} %compare_select_fusion, s32[256]{0:T(256)S(1)} %copy-done.1, s32[5120]{0:T(1024)S(1)} %multiply_add_fusion, f32[64,256]{1,0:T(8,128)S(1)} %copy-done), kind=kOutput, calls=%fused_computation.2 | convolution fusion | flops 183533568 | bytes 3364864 | tf_op jit(solution)/shard_map/dot_general | solution.py:63
  147.0 1.2 select_reduce_fusion
  148.9 0.4 fusion.13
  149.3 0.4 fusion.23
  150.5 0.4 fusion.12
  151.3 0.4 fusion.45
  152.0 0.4 fusion.47
  152.4 0.4 fusion.48
  153.2 0.4 fusion.50
  153.6 0.4 fusion.51
  154.4 0.4 fusion.43
  154.8 0.4 fusion.46
  155.1 0.4 fusion.49
  155.5 0.4 fusion.52
  156.2 0.9 fusion.14
  (26 shorter events, 2.7 us)
Async XLA Ops:
  7.2 84.1 %all-reduce.2.cloned.1.call-start = ((), (), s32[]{:S(2)}) async-start(), calls=%async_computation | async-start | bytes 131072 | tf_op jit(solution)/shard_map/psum | solution.py:52
  7.9 90.5 %copy-start.1 = (s32[256]{0:T(256)S(1)}, s32[256]{0:T(256)}, u32[]{:S(2)}) copy-start(s32[256]{0:T(256)} %param.5) | copy-start | bytes 3076
  33.7 88.9 %copy-start.2 = (bf16[1,64,5120]{2,1,0:T(8,128)(2,1)S(1)}, bf16[1,64,5120]{2,1,0:T(8,128)(2,1)}, u32[]{:S(2)}) copy-start(bf16[1,64,5120]{2,1,0:T(8,128)(2,1)} %param.4) | copy-start | bytes 1966084
  91.3 31.3 %copy-start = (f32[64,256]{1,0:T(8,128)S(1)}, f32[64,256]{1,0:T(8,128)}, u32[]{:S(2)}) copy-start(f32[64,256]{1,0:T(8,128)} %all-reduce.2.cloned.1.call-done) | copy-start | bytes 196612
  92.2 5.2 %collective-permute-start = (f32[64,256]{1,0:T(8,128)S(1)}, f32[64,256]{1,0:T(8,128)S(1)}, u32[]{:S(2)}, u32[]{:S(2)}) collective-permute-start(f32[64,256]{1,0:T(8,128)S(1)} %broadcast_multiply_fusion), channel_id=1, source_target_pairs={{0,1},{1,2},{2,3},{3,0},{4,5},{5,6},{6,7},{7,4},{8,9},{9,10},{10,1... | collective-permute-start | bytes 196616 | tf_op jit(solution)/shard_map/ppermute | solution.py:56
  97.4 23.1 %collective-permute-start.1 = (f32[64,256]{1,0:T(8,128)S(1)}, f32[64,256]{1,0:T(8,128)S(1)}, u32[]{:S(2)}, u32[]{:S(2)}) collective-permute-start(f32[64,256]{1,0:T(8,128)S(1)} %collective-permute-done), channel_id=1, source_target_pairs={{0,1},{1,2},{2,3},{3,0},{4,5},{5,6},{6,7},{7,4},{8,9},{9,10},{10,1... | collective-permute-start | bytes 196616 | tf_op jit(solution)/shard_map/ppermute | solution.py:56
  120.5 26.5 %collective-permute-start.2 = (f32[64,256]{1,0:T(8,128)S(1)}, f32[64,256]{1,0:T(8,128)S(1)}, u32[]{:S(2)}, u32[]{:S(2)}) collective-permute-start(f32[64,256]{1,0:T(8,128)S(1)} %collective-permute-done.1), channel_id=1, source_target_pairs={{0,1},{1,2},{2,3},{3,0},{4,5},{5,6},{6,7},{7,4},{8,9},{9,10},{10,1... | collective-permute-start | bytes 196616 | tf_op jit(solution)/shard_map/ppermute | solution.py:56
Sparse Core Ops, SparseCore 0:
  33.8 57.4 all-reduce.1
